TPU v7x, 512 devices: a whole 4x8x8 slice. The times are simulated.
512 devices in a mesh: leaf: 128 (over z, y, core), near: 4 (over x).
Axes of the slice: x: 4, y: 8, z: 8, core: 2. Of those that a mesh axis runs over, the one named last changes fastest.
Arguments:
- bases: float32 [1024, 64, 64], P('leaf'), may hold values from -1 to 4
- leaf_transfer: float32 [1024, 64, 64], P('leaf'), may hold values from -1 to 4
- top_transfer: float32 [512, 64, 64], P('leaf'), may hold values from -1 to 4
- couplings: bfloat16 [65536, 64, 64], P(('leaf', 'near')), may hold values from -6 to 6
- coupling_target: int32 [65536], P(('leaf', 'near')), may hold values from 0 to 7
- coupling_dest: int32 [65536, 1], P(('leaf', 'near')), may hold values from 0 to 127; in each aligned block of 128 rows (0 to 127, 128 to 255, ...) at most 2 rows name the same one
- coupling_local: int32 [65536], P(('leaf', 'near')), may hold values from 0 to 7
- top_couplings: bfloat16 [8192, 64, 64], P(('leaf', 'near')), may hold values from -0.59765625 to 0.59765625
- top_target: int32 [8192], P(('leaf', 'near')), may hold values from 0 to 7
- top_source: int32 [8192], P(('leaf', 'near')), may hold values from 0 to 255
Outputs:
- leaf_bases: float32 [1024, 64, 64], P(('leaf', 'near'))
- leaf_transfers: float32 [1024, 64, 64], P('leaf')
- top_transfers: float32 [512, 64, 64], P('leaf')
- new_couplings: bfloat16 [65536, 64, 64], P(('leaf', 'near'))
- new_top_couplings: bfloat16 [8192, 64, 64], P(('leaf', 'near'))
Inputs may be any that keep to these rules, and one draw needn't show every extreme that they name: `coupling_dest`: among the leaf blocks of one device, at most 2 have their source in the same subtree.
All inputs are finite; a program needn't handle non-finite values.
Results may differ from a plain program's by a relative error of at most 0.0065.
Values may be sent and summed in bfloat16 or wider, within the bound.
A program may use at most 128 MiB of HBM per device.

v0:
```python
import jax
import jax.numpy as jnp
from jax import lax
from jax.sharding import PartitionSpec as P

exact_mode = lax.Precision.HIGHEST


def swapped(value, axis, distance):
    mask = 2**distance
    pairs = [(source, source ^ mask) for source in range(lax.axis_size(axis))]
    return lax.ppermute(value, axis, pairs)


def gram_of(stacked):
    return jnp.einsum("nmk,nml->nkl", stacked, stacked, precision=exact_mode)


def right_solve(lower_part, stacked):

    def single(factor_one, block_one):
        return jax.scipy.linalg.solve_triangular(factor_one, block_one.T, lower=True).T

    return jax.vmap(single)(lower_part, stacked)


def on_device(
    bases,
    leaf_transfer,
    top_transfer,
    couplings,
    coupling_target,
    coupling_dest,
    coupling_local,
    top_couplings,
    top_target,
    top_source,
):
    leaves_here = bases.shape[0]
    rank_width = bases.shape[2]
    share = leaves_here // lax.axis_size("near")
    near_place = lax.axis_index("near")
    my_bases = lax.dynamic_slice_in_dim(bases, near_place * share, share, 0)
    lower_mine = jnp.linalg.cholesky(gram_of(my_bases))
    leaf_bases = right_solve(lower_mine, my_bases)
    leaf_factor = lax.all_gather(jnp.swapaxes(lower_mine, 1, 2), "near", axis=0, tiled=True)
    child_piece = jnp.einsum("nkr,nrl->nkl", leaf_factor, leaf_transfer, precision=exact_mode)
    sibling = swapped(child_piece, "leaf", 0)
    lower_middle = jnp.linalg.cholesky(gram_of(child_piece) + gram_of(sibling))
    leaf_transfers = right_solve(lower_middle, child_piece)
    mid_factor = jnp.swapaxes(lower_middle, 1, 2)
    leaf_place = lax.axis_index("leaf")
    parity = leaf_place % 2
    halfway = leaves_here // 2
    mid_mine = lax.dynamic_slice_in_dim(mid_factor, parity * halfway, halfway, 0)
    up_piece = jnp.einsum("nkr,nrl->nkl", mid_mine, top_transfer, precision=exact_mode)
    cousin = swapped(up_piece, "leaf", 1)
    lower_top = jnp.linalg.cholesky(gram_of(up_piece) + gram_of(cousin))
    top_transfers = right_solve(lower_top, up_piece)
    top_factor = jnp.swapaxes(lower_top, 1, 2)
    upper_bit = leaf_place // 2 % 2
    fourth = leaves_here // 4
    top_mine = lax.dynamic_slice_in_dim(top_factor, upper_bit * fourth, fourth, 0).astype(
        jnp.bfloat16
    )
    gathered = lax.all_gather(top_mine, "leaf", axis=0, tiled=True)
    quads = gathered.shape[0] // leaves_here
    top_table = gathered.reshape(quads, 2, 2, fourth, rank_width, rank_width)
    top_table = jnp.transpose(top_table, (0, 2, 1, 3, 4, 5)).reshape(
        quads * leaves_here, rank_width, rank_width
    )
    factor_low = leaf_factor.astype(jnp.bfloat16)
    target_rows = factor_low[coupling_target]
    halves = jnp.einsum(
        "nkr,nrl->nkl", target_rows, couplings, preferred_element_type=jnp.float32
    ).astype(jnp.bfloat16)
    destination = coupling_dest[:, 0]
    every_factor = lax.all_gather(factor_low, "leaf", axis=0, tiled=True)
    source_rows = every_factor[destination * leaves_here + coupling_local]
    new_couplings = jnp.einsum(
        "nkr,nlr->nkl", halves, source_rows, preferred_element_type=jnp.float32
    ).astype(jnp.bfloat16)
    quad_place = leaf_place // 4
    top_left = top_table[quad_place * leaves_here + top_target]
    top_right = top_table[top_source]
    half_top = jnp.einsum(
        "nkr,nrl->nkl", top_left, top_couplings, preferred_element_type=jnp.float32
    ).astype(jnp.bfloat16)
    new_top_couplings = jnp.einsum(
        "nkr,nlr->nkl", half_top, top_right, preferred_element_type=jnp.float32
    ).astype(jnp.bfloat16)
    return (leaf_bases, leaf_transfers, top_transfers, new_couplings, new_top_couplings)


def solution(mesh):
    in_specs = (
        P("leaf", None, None),
        P("leaf", None, None),
        P("leaf", None, None),
        P(("leaf", "near"), None, None),
        P(("leaf", "near")),
        P(("leaf", "near"), None),
        P(("leaf", "near")),
        P(("leaf", "near"), None, None),
        P(("leaf", "near")),
        P(("leaf", "near")),
    )
    out_specs = (
        P(("leaf", "near"), None, None),
        P("leaf", None, None),
        P("leaf", None, None),
        P(("leaf", "near"), None, None),
        P(("leaf", "near"), None, None),
    )
    return jax.shard_map(
        on_device, mesh=mesh, in_specs=in_specs, out_specs=out_specs, check_vma=False
    )
```

profile of v0, /device:TPU:1, one launch (start us, length us, event | category | flops | bytes accessed | tf_op | source)
XLA Modules:
  0.0 335.1 jit_solution(8678206649919999366)
XLA Ops:
  7.2 0.0 copy-start
  7.2 0.0 all-gather.5.cloned.1.call-start
  7.3 1.2 fusion.19
  8.5 0.1 copy.76
  8.6 11.7 %custom-call.24 = f32[2,64,64]{2,1,0:T(8,128)S(1)} custom-call(f32[2,64,64]{2,1,0:T(8,128)S(1)} %fusion.17), custom_call_target="Cholesky" | custom-call | tf_op jit(solution)/shard_map/jit(cholesky)/cholesky | solution.py:44
  20.4 0.1 compare_reduce_fusion.2
  20.5 0.1 fusion.21
  20.6 0.1 copy.78
  20.7 10.5 %all_gather.9 = f32[8,64,64]{2,1,0:T(8,128)S(1)} all-gather(f32[2,64,64]{2,1,0:T(8,128)S(1)} %copy.78), channel_id=1, replica_groups=mesh['leaf'=128,'near'=4] {'near'}, dimensions={0}, use_global_device_ids=true | all-gather | bytes 163840 | tf_op jit(solution)/shard_map/all_gather | solution.py:46
  31.2 1.3 fusion.26
  32.5 10.5 %collective-permute-start = (f32[8,64,64]{2,1,0:T(8,128)S(1)}, f32[8,64,64]{2,1,0:T(8,128)S(1)}, u32[]{:S(2)}, u32[]{:S(2)}) collective-permute-start(f32[8,64,64]{2,1,0:T(8,128)S(1)} %fusion.26), channel_id=1, source_target_pairs={{0,4},{4,0},{8,12},{12,8},{16,20},{20,16},{24,28},{28,24},{32,36},... | collective-permute-start | bytes 393224 | tf_op jit(solution)/shard_map/ppermute | solution.py:12
  43.1 0.0 copy-start.1
  43.1 0.6 fusion.27
  43.7 0.5 collective-permute-done
  44.2 0.6 convolution_add_fusion
  44.8 0.1 copy.83
  44.9 46.9 %custom-call.26 = f32[8,64,64]{2,1,0:T(8,128)S(1)} custom-call(f32[8,64,64]{2,1,0:T(8,128)S(1)} %fusion.9), custom_call_target="Cholesky" | custom-call | tf_op jit(solution)/shard_map/jit(cholesky)/cholesky | solution.py:49
  91.8 0.0 copy-start.2
  91.9 0.1 compare_reduce_fusion
  92.0 0.1 select_bitcast_fusion
  92.1 0.0 copy-done.1
  92.2 0.4 fusion.13
  92.5 1.9 collective-permute-start.1
  94.5 0.4 fusion.28
  94.9 4.3 %collective-permute-done.1 = f32[4,64,64]{2,1,0:T(8,128)S(1)} collective-permute-done((f32[4,64,64]{2,1,0:T(8,128)S(1)}, f32[4,64,64]{2,1,0:T(8,128)S(1)}, u32[]{:S(2)}, u32[]{:S(2)}) %collective-permute-start.1) | collective-permute-done | bytes 65568 | tf_op jit(solution)/shard_map/ppermute | solution.py:12
  99.1 0.4 convolution_add_fusion.1
  99.5 0.1 copy.90
  99.7 23.5 %custom-call.28 = f32[4,64,64]{2,1,0:T(8,128)S(1)} custom-call(f32[4,64,64]{2,1,0:T(8,128)S(1)} %fusion.12), custom_call_target="Cholesky" | custom-call | tf_op jit(solution)/shard_map/jit(cholesky)/cholesky | solution.py:58
  123.2 0.1 compare_reduce_fusion.1
  123.3 0.1 select_bitcast_fusion.1
  123.4 0.7 copy.93
  124.1 0.0 all-gather.5.cloned.1.call-update
  124.1 0.2 all-gather.3.cloned.1.call-start
  124.4 0.7 convert_element_type.21
  125.0 0.0 all-gather.3.cloned.1.call-update
  125.1 9.8 %custom-call.25 = f32[2,1,64,64]{2,3,1,0:T(8,128)S(1)} custom-call(f32[2,1,64,64]{3,2,1,0:T(8,128)S(1)} %get-tuple-element.30), custom_call_target="InvertDiagBlocksLowerTriangular" | custom-call | tf_op jit(solution)/shard_map/vmap(jit(_solve_triangular))/triangular_solve | solution.py:22
  134.9 0.0 copy-done.2
  135.0 1.9 gather_fusion
  136.8 0.0 copy-start.3
  136.8 0.0 copy-start.4
  136.9 0.0 copy-start.5
  136.9 0.0 copy-start.6
  136.9 4.7 %copy.92 = bf16[128,64,64]{2,1,0:T(8,128)(2,1)} copy(bf16[128,64,64]{0,2,1:T(8,128)(2,1)} %param.13) | data formatting | bytes 2097152 | tf_op args[3]
  141.6 0.0 copy-done.3
  141.6 0.0 copy-done.4
  141.7 0.0 copy-done.5
  141.7 0.0 copy-done.6
  141.7 1.7 fusion.15
  143.4 39.3 %custom-call.27 = f32[8,1,64,64]{2,3,1,0:T(8,128)S(1)} custom-call(f32[8,1,64,64]{3,2,1,0:T(8,128)S(1)} %get-tuple-element.27), custom_call_target="InvertDiagBlocksLowerTriangular" | custom-call | tf_op jit(solution)/shard_map/vmap(jit(_solve_triangular))/triangular_solve | solution.py:22
  182.7 1.1 fusion.7
  183.8 19.6 %custom-call.29 = f32[4,1,64,64]{2,3,1,0:T(8,128)S(1)} custom-call(f32[4,1,64,64]{3,2,1,0:T(8,128)S(1)} %get-tuple-element.25), custom_call_target="InvertDiagBlocksLowerTriangular" | custom-call | tf_op jit(solution)/shard_map/vmap(jit(_solve_triangular))/triangular_solve | solution.py:22
  203.4 0.9 fusion.10
  204.4 6.0 %all-gather.5.cloned.1.call-done = bf16[256,64,64]{2,1,0:T(8,128)(2,1)} async-done(((bf16[2,64,64]{2,1,0:T(8,128)(2,1)}), bf16[256,64,64]{2,1,0:T(8,128)(2,1)}) %all-gather.5.cloned.1.call-update) | async-done | bytes 2097168 | tf_op jit(solution)/shard_map/all_gather | solution.py:66
  210.3 6.0 %copy.94 = bf16[32,2,2,2,64,64]{5,4,3,1,2,0:T(8,128)(2,1)} copy(bf16[32,2,2,2,64,64]{5,4,3,2,1,0:T(8,128)(2,1)} %bitcast.60) | data formatting | bytes 4194304 | tf_op jit(solution)/shard_map/reshape | solution.py:68
  216.3 2.8 gather_fusion.3
  219.1 2.8 gather_fusion.2
  221.9 0.0 copy-done
  221.9 1.1 convolution_convert_fusion
  223.0 88.0 %all-gather.3.cloned.1.call-done = bf16[1024,64,64]{2,1,0:T(8,128)(2,1)} async-done(((bf16[8,64,64]{2,1,0:T(8,128)(2,1)}), bf16[1024,64,64]{2,1,0:T(8,128)(2,1)}) %all-gather.3.cloned.1.call-update) | async-done | bytes 8388624 | tf_op jit(solution)/shard_map/all_gather | solution.py:78
  311.0 7.9 %gather_fusion.1 = bf16[128,64,64]{2,1,0:T(8,128)(2,1)} fusion(bf16[1024,64,64]{2,1,0:T(8,128)(2,1)} %all-gather.3.cloned.1.call-done, s32[1024]{0:T(1024)S(1)} %pad_clamp_fusion.2), kind=kCustom, calls=%fused_computation.1 | custom fusion | bytes 2097664 | tf_op jit(solution)/shard_map/gather | solution.py:79
  318.9 5.3 %fusion.4 = bf16[128,64,64]{2,1,0:T(8,128)(2,1)} fusion(bf16[128,64,64]{2,1,0:T(8,128)(2,1)} %gather_fusion.1, bf16[128,64,64]{2,1,0:T(8,128)(2,1)S(1)} %gather_fusion, bf16[128,64,64]{2,1,0:T(8,128)(2,1)} %copy.92), kind=kOutput, calls=%fused_computation.7 | convolution fusion | flops 135266304 | bytes 4194304 | tf_op jit(solution)/shard_map/nkr,nlr->nkl/dot_general | solution.py:80
  324.3 4.0 %copy.95 = bf16[128,64,64]{0,2,1:T(8,128)(2,1)} copy(bf16[128,64,64]{2,1,0:T(8,128)(2,1)} %fusion.4) | data formatting | bytes 2097152
  (17 shorter events, 0.2 us)
Async XLA Ops:
  7.2 214.7 %copy-start = (bf16[16,64,64]{2,1,0:T(8,128)(2,1)S(1)}, bf16[16,64,64]{2,1,0:T(8,128)(2,1)}, u32[]{:S(2)}) copy-start(bf16[16,64,64]{2,1,0:T(8,128)(2,1)} %param.17) | copy-start | bytes 393220
  7.2 203.2 %all-gather.5.cloned.1.call-start = ((), (), s32[]{:S(2)}) async-start(), calls=%async_computation.1 | async-start | bytes 4227072 | tf_op jit(solution)/shard_map/all_gather | solution.py:66
  32.5 11.6 %collective-permute-start = (f32[8,64,64]{2,1,0:T(8,128)S(1)}, f32[8,64,64]{2,1,0:T(8,128)S(1)}, u32[]{:S(2)}, u32[]{:S(2)}) collective-permute-start(f32[8,64,64]{2,1,0:T(8,128)S(1)} %fusion.26), channel_id=1, source_target_pairs={{0,4},{4,0},{8,12},{12,8},{16,20},{20,16},{24,28},{28,24},{32,36},... | collective-permute-start | bytes 393224 | tf_op jit(solution)/shard_map/ppermute | solution.py:12
  43.1 49.1 %copy-start.1 = (f32[4,64,64]{2,1,0:T(8,128)S(1)}, f32[4,64,64]{2,1,0:T(8,128)}, u32[]{:S(2)}) copy-start(f32[4,64,64]{2,1,0:T(8,128)} %param.12) | copy-start | bytes 196612
  91.8 43.1 %copy-start.2 = (s32[128]{0:T(128)S(1)}, s32[128]{0:T(128)}, u32[]{:S(2)}) copy-start(s32[128]{0:T(128)} %param.14) | copy-start | bytes 1540
  92.5 6.6 %collective-permute-start.1 = (f32[4,64,64]{2,1,0:T(8,128)S(1)}, f32[4,64,64]{2,1,0:T(8,128)S(1)}, u32[]{:S(2)}, u32[]{:S(2)}) collective-permute-start(f32[4,64,64]{2,1,0:T(8,128)S(1)} %fusion.13), channel_id=1, source_target_pairs={{0,8},{4,12},{8,0},{12,4},{16,24},{20,28},{24,16},{28,20},{32,40},... | collective-permute-start | bytes 196616 | tf_op jit(solution)/shard_map/ppermute | solution.py:12
  124.1 186.9 %all-gather.3.cloned.1.call-start = ((), (), s32[]{:S(2)}) async-start(), calls=%async_computation | async-start | bytes 16908288 | tf_op jit(solution)/shard_map/all_gather | solution.py:78
  136.8 4.8 %copy-start.3 = (s32[16]{0:T(128)S(1)}, s32[16]{0:T(128)}, u32[]{:S(2)}) copy-start(s32[16]{0:T(128)} %param.19) | copy-start | bytes 196
  136.8 4.8 %copy-start.4 = (s32[128]{0:T(128)S(1)}, s32[128]{0:T(128)}, u32[]{:S(2)}) copy-start(s32[128]{0:T(128)} %param.16) | copy-start | bytes 1540
  136.9 4.8 %copy-start.5 = (s32[128,1]{0,1:T(1,128)S(1)}, s32[128,1]{0,1:T(1,128)}, u32[]{:S(2)}) copy-start(s32[128,1]{0,1:T(1,128)} %param.15) | copy-start | bytes 1540
  136.9 4.8 %copy-start.6 = (s32[16]{0:T(128)S(1)}, s32[16]{0:T(128)}, u32[]{:S(2)}) copy-start(s32[16]{0:T(128)} %param.18) | copy-start | bytes 196
Sparse Core Ops, SparseCore 0:
  124.3 86.0 all-gather.4
  214.0 96.9 all-gather.2
where the time goes:
time: 336 us; the launch traced here: 335 us
  other arithmetic  152 us (45%)
  waiting for transfers between devices  98.8 us (29%)
  local copies, waits for them, and re-layouts  31.3 us (9%)
  matrix products  15 us (4%)
  between operations  14.5 us (4%)
  starting transfers between devices  12.7 us (4%)
  blocking collectives  10.5 us (3%)
    all_gather x1, waiting for transfers between devices, on_device(): every_factor = lax.all_gather(factor_low, 'leaf', axis=0, tiled=True)  88 us
    another operation x6, other arithmetic, single(): jax.scipy.linalg.solve_triangular(factor_one, block_one.T, lower=True)  69 us
    another operation x3, other arithmetic, on_device(): lower_middle = jnp.linalg.cholesky(gram_of(child_piece) + gram_of(sibling))  47.1 us
    another operation x3, other arithmetic, on_device(): lower_top = jnp.linalg.cholesky(gram_of(up_piece) + gram_of(cousin))  23.6 us
    ppermute x2, starting transfers between devices, swapped(): return lax.ppermute(value, axis, pairs)  12.4 us
    another operation x4, other arithmetic, on_device(): lower_mine = jnp.linalg.cholesky(gram_of(my_bases))  11.9 us
    all_gather x1, blocking collectives, on_device(): lax.all_gather(jnp.swapaxes(lower_mine, 1, 2), 'near', axis=0, tiled=True)  10.5 us
    unnamed x16, local copies, waits for them, and re-layouts  8.83 us
  transfers between devices with their start and end apart: 4, of which 4 were waited for; matrix products, arithmetic and copies ran while one was open for 28% of the time, Pallas kernels for 0%

commit v1 on v0

v1 whole, which is shorter than its diff:
```python
import functools

import jax
import jax.numpy as jnp
from jax import lax
from jax.experimental import pallas as pl
from jax.experimental.pallas import tpu as pltpu
from jax.sharding import PartitionSpec as P

MESH = pl.DeviceIdType.MESH
F32 = jnp.float32
BF16 = jnp.bfloat16
EXACT = lax.Precision.HIGHEST
RING = 8


def tn(left, right, precision=EXACT):
    return lax.dot_general(
        left, right, (((0,), (0,)), ((), ())), precision=precision, preferred_element_type=F32
    )


def nn(left, right, precision=EXACT):
    return lax.dot_general(
        left, right, (((1,), (0,)), ((), ())), precision=precision, preferred_element_type=F32
    )


def nt(left, right, precision=EXACT):
    return lax.dot_general(
        left, right, (((1,), (1,)), ((), ())), precision=precision, preferred_element_type=F32
    )


def split_tn(piece, wide):
    def thirds(value):
        first = value.astype(BF16).astype(F32)
        rest = value - first
        second = rest.astype(BF16).astype(F32)
        return first, second, rest - second

    a1, a2, a3 = thirds(piece)
    b1, b2, b3 = thirds(wide)
    left = jnp.concatenate([a1, a1, a2, a1, a2, a3], 0).astype(BF16)
    right = jnp.concatenate([b1, b2, b1, b3, b2, b1], 0).astype(BF16)
    return tn(left, right, None)


def eliminate_panel(work, first, count, panel):
    depth = 8
    start = depth * panel
    group = pl.ds(first, count)
    row_at = lax.broadcasted_iota(jnp.int32, (count, depth, 128), 1)
    rows = work[group, start : start + depth, :]
    columns = [
        jnp.broadcast_to(rows[:, :, start + j : start + j + 1], (count, depth, 128))
        for j in range(depth)
    ]
    scale = jnp.zeros((count, depth, 128), F32)
    for j in range(depth):
        column = columns[j]
        pivot = jnp.broadcast_to(column[:, j : j + 1, :], (count, depth, 128))
        scale = jnp.where(row_at == j, lax.rsqrt(pivot), scale)
        if j < depth - 1:
            share = jnp.where(row_at > j, column / pivot, 0.0)
            rows = rows - share * rows[:, j : j + 1, :]
            for k in range(j + 1, depth):
                columns[k] = columns[k] - share * columns[k][:, j : j + 1, :]
    done = rows * scale
    work[group, start : start + depth, :] = done
    after = start + depth
    if after < 64:
        for n in range(count):
            update = split_tn(done[n][:, :64], done[n])
            work[first + n, after:, :] = work[first + n, after:, :] - update[after:, :]


def kernel(
    bases,
    leaf_transfer,
    top_transfer,
    couplings,
    top_couplings,
    coupling_target,
    coupling_dest,
    coupling_local,
    top_target,
    top_source,
    leaf_bases,
    leaf_transfers,
    top_transfers,
    new_couplings,
    new_top,
    work,
    h_mine,
    h_theirs,
    k_mine,
    k_theirs,
    table,
    top_table,
    stacked,
    blocks,
    halves,
    pair_sem,
    a_send,
    a_recv,
    b_send,
    b_recv,
    s_send,
    s_recv,
    ta_send,
    ta_recv,
    tb_send,
    tb_recv,
    ts_send,
    ts_recv,
):
    me = lax.axis_index("leaf")
    near = lax.axis_index("near")
    core = me % 2
    y = (me // 2) % RING
    z = me // (2 * RING)
    a = z + core * (y - z)
    b = y + core * (z - y)

    def device(a_at, b_at):
        first = a_at + core * (b_at - a_at)
        second = b_at + core * (a_at - b_at)
        return {"leaf": (first * RING + second) * 2 + core}

    def wrap(value):
        return (value + 2 * RING) % RING

    a_right, a_left = device(wrap(a + 1), b), device(wrap(a - 1), b)
    b_right, b_left = device(a, wrap(b + 1)), device(a, wrap(b - 1))
    sibling = {"leaf": me + 1 - 2 * core}
    cousin = {"leaf": me + 2 - 4 * ((me // 2) % 2)}
    parity = core
    upper = (me // 2) % 2

    barrier = pltpu.get_barrier_semaphore()
    for neighbour in (a_right, a_left, b_right, b_left, sibling):
        pl.semaphore_signal(barrier, inc=1, device_id=neighbour, device_id_type=MESH)
    pl.semaphore_wait(barrier, 5)

    def remote(source, target, send, recv, to):
        return pltpu.make_async_remote_copy(
            src_ref=source,
            dst_ref=target,
            send_sem=send,
            recv_sem=recv,
            device_id=to,
            device_id_type=MESH,
        )

    def row_of(b_at, a_at):
        return core * 64 + b_at * RING + a_at

    def leaf_span(b_at, a_at, low, high):
        return table.at[pl.ds(row_of(b_at, a_at) * 4 + low, high - low)]

    started = []

    def go(copy):
        copy.start()
        started.append(copy)

    row = lax.broadcasted_iota(jnp.int32, (64, 128), 0)
    lane = lax.broadcasted_iota(jnp.int32, (64, 128), 1)
    keep = row <= lane % 64
    low_lane = lane < 64
    unit = jnp.where(row == lane - 64, 1.0, 0.0)

    for n in range(20):
        work[n] = unit
    for n in range(8):
        gram = tn(bases[n], bases[n])
        work[n, :, 0:64] = gram
        h_mine[n] = tn(leaf_transfer[n], nn(gram, leaf_transfer[n]))
    to_sibling = remote(h_mine, h_theirs, pair_sem.at[0], pair_sem.at[1], sibling)
    to_sibling.start()

    for panel in range(4):
        eliminate_panel(work, 0, 8, panel)

    to_sibling.wait()
    for n in range(8):
        work[8 + n, :, 0:64] = h_mine[n] + h_theirs[n]
    for n in range(4):
        mid = work[8 + parity * 4 + n][:, 0:64]
        k_mine[n] = tn(top_transfer[n], nn(mid, top_transfer[n]))
    to_cousin = remote(k_mine, k_theirs, pair_sem.at[2], pair_sem.at[3], cousin)
    to_cousin.start()

    for panel in range(4, 8):
        eliminate_panel(work, 0, 8, panel)

    def pair_of(first, second):
        both = jnp.where(low_lane, first, pltpu.roll(second, 64, 1))
        return jnp.where(keep, both, 0.0).astype(BF16)

    for q in range(4):
        table[row_of(b, a) * 4 + q] = pair_of(work[2 * q], work[2 * q + 1])

    def a_copy(k, way):
        at = wrap(a - way * k)
        low, high = (0, 4) if k < 3 else ((0, 2) if way > 0 else (2, 4))
        lane_at = k if way > 0 else 4 + k
        return remote(
            leaf_span(b, at, low, high),
            leaf_span(b, at, low, high),
            a_send.at[lane_at],
            a_recv.at[lane_at],
            a_right if way > 0 else a_left,
        )

    def a_arrival(k, way):
        at = wrap(a - way * k)
        low, high = (0, 4) if k < 4 else ((0, 2) if way > 0 else (2, 4))
        lane_at = k - 1 if way > 0 else 3 + k
        span = leaf_span(b, at, low, high)
        return remote(span, span, a_send.at[lane_at], a_recv.at[lane_at], sibling)

    offsets = [0, 1, -1, 2, -2, 3, -3, 4]

    def b_copy(h, w, way):
        b_at, a_at = wrap(b - way * h), wrap(a - offsets[w])
        low, high = (0, 4) if h < 3 else ((0, 2) if way > 0 else (2, 4))
        span = leaf_span(b_at, a_at, low, high)
        lane_at = (h if way > 0 else 4 + h) * 8 + w
        return remote(
            span, span, b_send.at[lane_at], b_recv.at[lane_at], b_right if way > 0 else b_left
        )

    def b_arrival(h, w, way):
        b_at, a_at = wrap(b - way * h), wrap(a - offsets[w])
        low, high = (0, 4) if h < 4 else ((0, 2) if way > 0 else (2, 4))
        span = leaf_span(b_at, a_at, low, high)
        lane_at = (h - 1 if way > 0 else 3 + h) * 8 + w
        return remote(span, span, b_send.at[lane_at], b_recv.at[lane_at], sibling)

    def s_copy(b_at, slot):
        span = table.at[pl.ds(row_of(b_at, 0) * 4, 32)]
        return remote(span, span, s_send.at[slot], s_recv.at[slot], sibling)

    def s_arrival(b_offset, slot):
        at = wrap(a + b_offset)
        span = table.at[pl.ds(((1 - core) * 64 + at * RING) * 4, 32)]
        return remote(span, span, s_send.at[slot], s_recv.at[slot], sibling)

    b_offsets = [0, -1, 1, -2, 2, -3, 3, 4]

    def leaf_event(h, w):
        if h == 0:
            if w == 0:
                go(a_copy(0, 1))
                go(a_copy(0, -1))
            elif w < 7:
                way = 1 if offsets[w] > 0 else -1
                k = abs(offsets[w])
                a_arrival(k, way).wait_recv()
                go(a_copy(k, way))
            else:
                a_arrival(4, 1).wait_recv()
                a_arrival(4, -1).wait_recv()
            go(b_copy(0, w, 1))
            go(b_copy(0, w, -1))
        else:
            b_arrival(h, w, 1).wait_recv()
            b_arrival(h, w, -1).wait_recv()
            if h < 4:
                go(b_copy(h, w, 1))
                go(b_copy(h, w, -1))
        if w == 7:
            for slot, offset in enumerate(b_offsets):
                if abs(offset) == h:
                    go(s_copy(wrap(b + offset), slot))

    def top_a_copy(k, way):
        at = wrap(a - way * k)
        lane_at = k if way > 0 else 4 + k
        span = top_table.at[row_of(b, at)]
        return remote(
            span, span, ta_send.at[lane_at], ta_recv.at[lane_at], a_right if way > 0 else a_left
        )

    def top_a_arrival(k, way):
        at = wrap(a - way * k)
        lane_at = k - 1 if way > 0 else 3 + k
        span = top_table.at[row_of(b, at)]
        return remote(span, span, ta_send.at[lane_at], ta_recv.at[lane_at], sibling)

    def top_b_span(b_at, h, way):
        low, size = (0, 8) if h < 4 else ((0, 4) if way > 0 else (4, 4))
        return top_table.at[pl.ds(row_of(b_at, 0) + low, size)]

    def top_b_copy(h, way):
        span = top_b_span(wrap(b - way * h), h + 1, way)
        lane_at = h if way > 0 else 4 + h
        return remote(
            span, span, tb_send.at[lane_at], tb_recv.at[lane_at], b_right if way > 0 else b_left
        )

    def top_b_arrival(h, way):
        span = top_b_span(wrap(b - way * h), h, way)
        lane_at = h - 1 if way > 0 else 3 + h
        return remote(span, span, tb_send.at[lane_at], tb_recv.at[lane_at], sibling)

    def top_s_copy(b_at, slot):
        span = top_table.at[pl.ds(row_of(b_at, 0), 8)]
        return remote(span, span, ts_send.at[slot], ts_recv.at[slot], sibling)

    def top_s_arrival(b_offset, slot):
        at = wrap(a + b_offset)
        span = top_table.at[pl.ds((1 - core) * 64 + at * RING, 8)]
        return remote(span, span, ts_send.at[slot], ts_recv.at[slot], sibling)

    def top_first():
        first = work[16 + upper * 2]
        second = work[17 + upper * 2]
        top_table[row_of(b, a)] = pair_of(first, second)
        go(top_a_copy(0, 1))
        go(top_a_copy(0, -1))

    def top_along_a(k):
        top_a_arrival(k, 1).wait_recv()
        if k < 4:
            top_a_arrival(k, -1).wait_recv()
            go(top_a_copy(k, 1))
            if k < 3:
                go(top_a_copy(k, -1))

    def top_along_b(h):
        if h > 0:
            top_b_arrival(h, 1).wait_recv()
            top_b_arrival(h, -1).wait_recv()
        if h < 4:
            go(top_b_copy(h, 1))
            go(top_b_copy(h, -1))
        for slot, offset in enumerate(b_offsets):
            if abs(offset) == h:
                go(top_s_copy(wrap(b + offset), slot))

    top_events = (
        [top_first]
        + [functools.partial(top_along_a, k) for k in range(1, 5)]
        + [functools.partial(top_along_b, h) for h in range(5)]
    )

    def top_gram():
        to_cousin.wait()
        for n in range(4):
            work[16 + n, :, 0:64] = k_mine[n] + k_theirs[n]

    def factor(n):
        return jnp.where(keep, work[n], 0.0)[:, 0:64]

    def inverse_transposed(n):
        return work[n][:, 64:128]

    def finish_bases():
        for k in range(2):
            at = near * 2 + k
            leaf_bases[k] = nt(bases[at], inverse_transposed(at))

    def finish_leaf(n):
        piece = nn(factor(n), leaf_transfer[n])
        leaf_transfers[n] = nt(piece, inverse_transposed(8 + n))

    def finish_top(n):
        piece = nn(factor(8 + parity * 4 + n), top_transfer[n])
        top_transfers[n] = nt(piece, inverse_transposed(16 + n))

    def stack_factors():
        for n in range(8):
            low = factor(n).astype(BF16)
            stacked[n] = jnp.concatenate([low[:, :32], low[:, 32:]], 0)

    def unpack_blocks(first, last):
        for k in range(first, last):
            slab = jnp.concatenate(
                [couplings[k].astype(F32), couplings[k + 32].astype(F32)], 0
            )
            blocks[pl.ds(k, 128, stride=32), :] = jnp.transpose(slab)

    def half_step(first, last):
        for n in range(first, last):
            block = blocks[32 * n : 32 * n + 32, :].astype(BF16)
            both = nn(stacked[coupling_target[n]], block, None)
            mixed = jnp.where(low_lane, both[0:64], both[64:128])
            mixed = mixed + pltpu.roll(mixed, 64, 1)
            odd = coupling_local[n] & 1
            here = (lane // 64) == odd
            halves[n] = jnp.where(here, mixed, 0.0).astype(BF16)

    tasks = [top_gram]
    tasks += [functools.partial(eliminate_panel, work, 8, 12, panel) for panel in range(8)]
    late = [stack_factors, finish_bases]
    late += [functools.partial(unpack_blocks, k, k + 4) for k in range(0, 32, 4)]
    late += [functools.partial(half_step, n, n + 16) for n in range(0, 128, 16)]
    late += [functools.partial(finish_leaf, n) for n in range(8)]
    late += [functools.partial(finish_top, n) for n in range(4)]

    events = [functools.partial(leaf_event, h, w) for h in range(5) for w in range(8)]
    tops_at = {9: 0, 12: 1, 15: 2, 18: 3, 21: 4, 22: 5, 26: 6, 30: 7, 34: 8, 39: 9}
    queue = tasks + late
    for place, event in enumerate(events):
        event()
        if place in tops_at:
            top_events[tops_at[place]]()
        if queue:
            queue.pop(0)()
    while queue:
        queue.pop(0)()

    for slot, offset in enumerate(b_offsets):
        top_s_arrival(offset, slot).wait_recv()
        s_arrival(offset, slot).wait_recv()

    def table_row(leaf_place):
        c = leaf_place & 1
        y_at = (leaf_place >> 1) & 7
        z_at = leaf_place >> 4
        return c * 64 + (y_at + c * (z_at - y_at)) * RING + z_at + c * (y_at - z_at)

    quad = me // 4

    def top_tile(cluster):
        place = (cluster >> 3) * 4 + (cluster & 2) + ((cluster >> 2) & 1)
        return top_table[table_row(place)]

    for n in range(16):
        target = quad * 8 + top_target[n]
        source = top_source[n]
        left = jnp.where((lane // 64) == (target & 1), top_tile(target), jnp.zeros((), BF16))
        block = top_couplings[n]
        double = jnp.concatenate([block, block], 1)
        half = nn(left, jnp.concatenate([double, double], 0), None)
        half = jnp.where((lane // 64) == (source & 1), half, 0.0).astype(BF16)
        new_top[n] = nt(half, top_tile(source), None).astype(BF16)

    for n in range(128):
        place = table_row(coupling_dest[n]) * 4 + (coupling_local[n] >> 1)
        new = nt(halves[n], table[place], None)
        blocks[32 * n : 32 * n + 32, :] = jnp.concatenate([new[0:32], new[32:64]], 1)
    for k in range(32):
        slab = jnp.transpose(blocks[pl.ds(k, 128, stride=32), :]).astype(BF16)
        new_couplings[k] = slab[0:64]
        new_couplings[k + 32] = slab[64:128]

    for copy in started:
        copy.wait_send()


def on_device(
    bases,
    leaf_transfer,
    top_transfer,
    couplings,
    coupling_target,
    coupling_dest,
    coupling_local,
    top_couplings,
    top_target,
    top_source,
):
    vmem = pl.BlockSpec(memory_space=pltpu.VMEM)
    smem = pl.BlockSpec(memory_space=pltpu.SMEM)
    dma = pltpu.SemaphoreType.DMA
    leaf_bases, leaf_transfers, top_transfers, new_couplings, new_top = pl.pallas_call(
        kernel,
        out_shape=(
            jax.ShapeDtypeStruct((2, 64, 64), F32),
            jax.ShapeDtypeStruct((8, 64, 64), F32),
            jax.ShapeDtypeStruct((4, 64, 64), F32),
            jax.ShapeDtypeStruct((64, 64, 128), BF16),
            jax.ShapeDtypeStruct((16, 64, 64), BF16),
        ),
        in_specs=[vmem] * 5 + [smem] * 5,
        out_specs=[vmem] * 5,
        scratch_shapes=[
            pltpu.VMEM((20, 64, 128), F32),
            pltpu.VMEM((8, 64, 64), F32),
            pltpu.VMEM((8, 64, 64), F32),
            pltpu.VMEM((4, 64, 64), F32),
            pltpu.VMEM((4, 64, 64), F32),
            pltpu.VMEM((512, 64, 128), BF16),
            pltpu.VMEM((128, 64, 128), BF16),
            pltpu.VMEM((8, 128, 32), BF16),
            pltpu.VMEM((4096, 128), F32),
            pltpu.VMEM((128, 64, 128), BF16),
            dma((4,)),
            dma((8,)),
            dma((8,)),
            dma((64,)),
            dma((64,)),
            dma((8,)),
            dma((8,)),
            dma((8,)),
            dma((8,)),
            dma((8,)),
            dma((8,)),
            dma((8,)),
            dma((8,)),
        ],
        compiler_params=pltpu.CompilerParams(
            collective_id=0, has_side_effects=True, vmem_limit_bytes=40 * 2**20
        ),
    )(
        bases,
        leaf_transfer,
        top_transfer,
        jnp.transpose(couplings, (1, 2, 0)),
        top_couplings,
        coupling_target,
        coupling_dest[:, 0],
        coupling_local,
        top_target,
        top_source,
    )
    return (
        leaf_bases,
        leaf_transfers,
        top_transfers,
        jnp.transpose(new_couplings, (2, 0, 1)),
        new_top,
    )


def solution(mesh):
    in_specs = (
        P("leaf", None, None),
        P("leaf", None, None),
        P("leaf", None, None),
        P(("leaf", "near"), None, None),
        P(("leaf", "near")),
        P(("leaf", "near"), None),
        P(("leaf", "near")),
        P(("leaf", "near"), None, None),
        P(("leaf", "near")),
        P(("leaf", "near")),
    )
    out_specs = (
        P(("leaf", "near"), None, None),
        P("leaf", None, None),
        P("leaf", None, None),
        P(("leaf", "near"), None, None),
        P(("leaf", "near"), None, None),
    )
    return jax.shard_map(
        on_device, mesh=mesh, in_specs=in_specs, out_specs=out_specs, check_vma=False
    )
```

time: 336 us -> 85.3 us (0.25)
  other arithmetic: 152 us -> 0 us
  waiting for transfers between devices: 98.8 us -> 0 us
  Pallas kernels: 0 us -> 75 us
  local copies, waits for them, and re-layouts: 31.3 us -> 9.31 us
  matrix products: 15 us -> 0 us
  between operations: 14.5 us -> 0.69 us
  starting transfers between devices: 12.7 us -> 0 us
  blocking collectives: 10.5 us -> 0 us
    another operation x16 -> x0, other arithmetic: 152 us -> none  [the longest x6 69 us: single(): jax.scipy.linalg.solve_triangular(factor_one, block_one.T, lower=True)]
    all_gather x2 -> x0, waiting for transfers between devices: 94 us -> none  [the longest x1 88 us: on_device(): every_factor = lax.all_gather(factor_low, 'leaf', axis=0, tiled=True)]
    pallas_call x0 -> x1, Pallas kernels: none -> 75 us  [on_device(): pl.pallas_call(kernel, out_shape=(jax.ShapeDtypeStruct((2, 64, 64), F32),...]
    gather x4 -> x0, local copies, waits for them, and re-layouts: 15.4 us -> none  [the longest x1 7.93 us: on_device(): source_rows = every_factor[destination * leaves_here + coupling_local]]
    ppermute x2 -> x0, starting transfers between devices: 12.4 us -> none  [swapped(): return lax.ppermute(value, axis, pairs)]
    dot_general x9 -> x0, matrix products: 11.3 us -> none  [the longest x1 5.34 us: on_device(): jnp.einsum('nkr,nlr->nkl', halves, source_rows, preferred_element_type=jn...]
    all_gather x1 -> x0, blocking collectives: 10.5 us -> none  [on_device(): lax.all_gather(jnp.swapaxes(lower_mine, 1, 2), 'near', axis=0, tiled=True)]
    reshape x1 -> x0, local copies, waits for them, and re-layouts: 5.99 us -> none  [on_device(): top_table = gathered.reshape(quads, 2, 2, fourth, rank_width, rank_width)]
  transfers between devices with their start and end apart: 4 -> 0, of which waited for: 4 -> 0; matrix products, arithmetic and copies ran while one was open for 28% -> 0% of each run, Pallas kernels for 0% -> 0%
where the time goes in v1:
time: 85.3 us; the launch traced here: 85 us
  Pallas kernels  75 us (88%)
  local copies, waits for them, and re-layouts  9.31 us (11%)
    pallas_call x1, Pallas kernels, on_device(): pl.pallas_call(kernel, out_shape=(jax.ShapeDtypeStruct((2, 64, 64), F32),...  75 us
    unnamed x25, local copies, waits for them, and re-layouts  9.31 us

profile of v1, /device:TPU:1, one launch (start us, length us, event | category | flops | bytes accessed | tf_op | source)
XLA Modules:
  0.0 85.0 jit_solution(6163137366018117253)
XLA Ops:
  0.6 0.0 copy-start.8
  0.6 0.0 copy-start.9
  0.7 0.0 copy-start.5
  0.7 0.0 copy-start.6
  0.7 0.0 copy-start.7
  0.7 0.6 copy-done.8
  1.3 0.0 copy-done.9
  1.3 0.0 copy-done.5
  1.3 0.0 copy-done.6
  1.3 0.0 copy-done.7
  1.4 0.0 copy-start
  1.4 1.2 %copy-done = bf16[128,64,64]{0,2,1:T(8,128)(2,1)S(1)} copy-done((bf16[128,64,64]{0,2,1:T(8,128)(2,1)S(1)}, bf16[128,64,64]{0,2,1:T(8,128)(2,1)}, u32[]{:S(2)}) %copy-start) | copy-done | bytes 1048600
  2.6 0.0 copy-start.1
  2.6 0.9 %copy-done.1 = f32[8,64,64]{2,1,0:T(8,128)S(1)} copy-done((f32[8,64,64]{2,1,0:T(8,128)S(1)}, f32[8,64,64]{2,1,0:T(8,128)}, u32[]{:S(2)}) %copy-start.1) | copy-done | bytes 131096
  3.5 0.0 copy-start.2
  3.5 0.9 %copy-done.2 = f32[8,64,64]{2,1,0:T(8,128)S(1)} copy-done((f32[8,64,64]{2,1,0:T(8,128)S(1)}, f32[8,64,64]{2,1,0:T(8,128)}, u32[]{:S(2)}) %copy-start.2) | copy-done | bytes 131096
  4.5 0.0 copy-start.3
  4.5 0.9 %copy-done.3 = bf16[16,64,64]{2,1,0:T(8,128)(2,1)S(1)} copy-done((bf16[16,64,64]{2,1,0:T(8,128)(2,1)S(1)}, bf16[16,64,64]{2,1,0:T(8,128)(2,1)}, u32[]{:S(2)}) %copy-start.3) | copy-done | bytes 131096
  5.4 0.0 copy-start.4
  5.4 0.9 %copy-done.4 = f32[4,64,64]{2,1,0:T(8,128)S(1)} copy-done((f32[4,64,64]{2,1,0:T(8,128)S(1)}, f32[4,64,64]{2,1,0:T(8,128)}, u32[]{:S(2)}) %copy-start.4) | copy-done | bytes 65560
  6.3 75.0 %shard_map.137 = (f32[2,64,64]{2,1,0:T(8,128)S(1)}, f32[8,64,64]{2,1,0:T(8,128)S(1)}, f32[4,64,64]{2,1,0:T(8,128)S(1)}, bf16[64,64,128]{2,1,0:T(8,128)(2,1)S(1)}, bf16[16,64,64]{2,1,0:T(8,128)(2,1)S(1)}) custom-call(f32[8,64,64]{2,1,0:T(8,128)S(1)} %copy-done.1, f32[8,64,64]{2,1,0:T(8,128)S(1)} %copy-done.2, f32[4,64,64]{2,1,0:T(8,128)S(1)} %copy-done.4, ...), custom_call_target="tpu_custom_call" | custom-call | tf_op jit(solution)/shard_map/pallas_call | solution.py:470
  81.3 0.6 copy.20
  81.9 0.7 copy.21
  82.6 0.7 copy.22
  83.3 1.0 %copy.23 = bf16[128,64,64]{0,2,1:T(8,128)(2,1)} copy(bf16[128,64,64]{0,2,1:T(8,128)(2,1)S(1)} %bitcast.4) | data formatting | bytes 2097152
  84.3 0.7 copy.24
Async XLA Ops:
  0.6 0.7 copy-start.8
  0.6 0.7 copy-start.9
  0.7 0.7 copy-start.5
  0.7 0.7 copy-start.6
  0.7 0.7 copy-start.7
  1.4 1.2 %copy-start = (bf16[128,64,64]{0,2,1:T(8,128)(2,1)S(1)}, bf16[128,64,64]{0,2,1:T(8,128)(2,1)}, u32[]{:S(2)}) copy-start(bf16[128,64,64]{0,2,1:T(8,128)(2,1)} %param.13) | copy-start | bytes 3145732
  2.6 0.9 %copy-start.1 = (f32[8,64,64]{2,1,0:T(8,128)S(1)}, f32[8,64,64]{2,1,0:T(8,128)}, u32[]{:S(2)}) copy-start(f32[8,64,64]{2,1,0:T(8,128)} %bases.1) | copy-start | bytes 393220
  3.5 0.9 %copy-start.2 = (f32[8,64,64]{2,1,0:T(8,128)S(1)}, f32[8,64,64]{2,1,0:T(8,128)}, u32[]{:S(2)}) copy-start(f32[8,64,64]{2,1,0:T(8,128)} %leaf_transfer.1) | copy-start | bytes 393220
  4.5 0.9 %copy-start.3 = (bf16[16,64,64]{2,1,0:T(8,128)(2,1)S(1)}, bf16[16,64,64]{2,1,0:T(8,128)(2,1)}, u32[]{:S(2)}) copy-start(bf16[16,64,64]{2,1,0:T(8,128)(2,1)} %top_couplings.1) | copy-start | bytes 393220
  5.4 0.9 %copy-start.4 = (f32[4,64,64]{2,1,0:T(8,128)S(1)}, f32[4,64,64]{2,1,0:T(8,128)}, u32[]{:S(2)}) copy-start(f32[4,64,64]{2,1,0:T(8,128)} %top_transfer.1) | copy-start | bytes 196612

commit v2 on v1

v2 whole, which is shorter than its diff:
```python
import functools

import jax
import jax.numpy as jnp
from jax import lax
from jax.experimental import pallas as pl
from jax.experimental.pallas import tpu as pltpu
from jax.sharding import PartitionSpec as P

MESH = pl.DeviceIdType.MESH
F32 = jnp.float32
BF16 = jnp.bfloat16
EXACT = lax.Precision.HIGHEST
RING = 8


def tn(left, right, precision=EXACT):
    return lax.dot_general(
        left, right, (((0,), (0,)), ((), ())), precision=precision, preferred_element_type=F32
    )


def nn(left, right, precision=EXACT):
    return lax.dot_general(
        left, right, (((1,), (0,)), ((), ())), precision=precision, preferred_element_type=F32
    )


def nt(left, right, precision=EXACT):
    return lax.dot_general(
        left, right, (((1,), (1,)), ((), ())), precision=precision, preferred_element_type=F32
    )


def split_tn(piece, wide):
    def thirds(value):
        first = value.astype(BF16).astype(F32)
        rest = value - first
        second = rest.astype(BF16).astype(F32)
        return first, second, rest - second

    a1, a2, a3 = thirds(piece)
    b1, b2, b3 = thirds(wide)
    left = jnp.concatenate([a1, a1, a2, a1, a2, a3], 0).astype(BF16)
    right = jnp.concatenate([b1, b2, b1, b3, b2, b1], 0).astype(BF16)
    return tn(left, right, None)


def eliminate_panel(work, first, count, panel):
    depth = 8
    start = depth * panel
    group = pl.ds(first, count)
    row_at = lax.broadcasted_iota(jnp.int32, (count, depth, 128), 1)
    rows = work[group, start : start + depth, :]
    columns = [
        jnp.broadcast_to(rows[:, :, start + j : start + j + 1], (count, depth, 128))
        for j in range(depth)
    ]
    scale = jnp.zeros((count, depth, 128), F32)
    for j in range(depth):
        column = columns[j]
        pivot = jnp.broadcast_to(column[:, j : j + 1, :], (count, depth, 128))
        scale = jnp.where(row_at == j, lax.rsqrt(pivot), scale)
        if j < depth - 1:
            share = jnp.where(row_at > j, column / pivot, 0.0)
            rows = rows - share * rows[:, j : j + 1, :]
            for k in range(j + 1, depth):
                columns[k] = columns[k] - share * columns[k][:, j : j + 1, :]
    done = rows * scale
    work[group, start : start + depth, :] = done
    after = start + depth
    if after < 64:
        for n in range(count):
            update = split_tn(done[n][:, :64], done[n])
            work[first + n, after:, :] = work[first + n, after:, :] - update[after:, :]


def kernel(
    bases_in,
    leaf_transfer_in,
    top_transfer_in,
    couplings_in,
    top_couplings_in,
    coupling_target_in,
    coupling_dest_in,
    coupling_local_in,
    top_target_in,
    top_source_in,
    leaf_bases,
    leaf_transfers,
    top_transfers,
    new_couplings,
    new_top,
    bases,
    leaf_transfer,
    top_transfer,
    couplings,
    top_couplings,
    coupling_target,
    coupling_dest,
    coupling_local,
    top_target,
    top_source,
    work,
    h_mine,
    h_theirs,
    k_mine,
    k_theirs,
    table,
    top_table,
    stacked,
    blocks,
    halves,
    in_sem,
    pair_sem,
    a_send,
    a_recv,
    ta_send,
    ta_recv,
    b_send,
    b_recv,
    s_send,
    s_recv,
):
    loads = [
        pltpu.make_async_copy(source, target, in_sem.at[n])
        for n, (source, target) in enumerate(
            [
                (bases_in, bases),
                (leaf_transfer_in, leaf_transfer),
                (top_transfer_in, top_transfer),
                (couplings_in, couplings),
                (top_couplings_in, top_couplings),
                (coupling_target_in, coupling_target),
                (coupling_dest_in, coupling_dest),
                (coupling_local_in, coupling_local),
                (top_target_in, top_target),
                (top_source_in, top_source),
            ]
        )
    ]
    for copy in loads:
        copy.start()

    me = lax.axis_index("leaf")
    near = lax.axis_index("near")
    core = me % 2
    y = (me // 2) % RING
    z = me // (2 * RING)
    a = z + core * (y - z)
    b = y + core * (z - y)

    def device(a_at, b_at):
        first = a_at + core * (b_at - a_at)
        second = b_at + core * (a_at - b_at)
        return {"leaf": (first * RING + second) * 2 + core}

    def wrap(value):
        return (value + 2 * RING) % RING

    b_right, b_left = device(a, wrap(b + 1)), device(a, wrap(b - 1))
    sibling = {"leaf": me + 1 - 2 * core}
    cousin = {"leaf": me + 2 - 4 * ((me // 2) % 2)}
    parity = core
    upper = (me // 2) % 2

    barrier = pltpu.get_barrier_semaphore()
    partners = [sibling, b_right, b_left] + [device(wrap(a + k), b) for k in range(1, RING)]
    for partner in partners:
        pl.semaphore_signal(barrier, inc=1, device_id=partner, device_id_type=MESH)
    pl.semaphore_wait(barrier, len(partners))

    def remote(source, target, send, recv, to):
        return pltpu.make_async_remote_copy(
            src_ref=source,
            dst_ref=target,
            send_sem=send,
            recv_sem=recv,
            device_id=to,
            device_id_type=MESH,
        )

    def row_of(b_at, a_at):
        return core * 64 + b_at * RING + a_at

    started = []

    def go(copy):
        copy.start()
        started.append(copy)

    row = lax.broadcasted_iota(jnp.int32, (64, 128), 0)
    lane = lax.broadcasted_iota(jnp.int32, (64, 128), 1)
    keep = row <= lane % 64
    low_lane = lane < 64
    unit = jnp.where(row == lane - 64, 1.0, 0.0)
    row32 = lax.broadcasted_iota(jnp.int32, (32, 128), 0)
    lane32 = lax.broadcasted_iota(jnp.int32, (32, 128), 1)

    for n in range(20):
        work[n] = unit
    loads[0].wait()
    loads[1].wait()
    for n in range(8):
        gram = tn(bases[n], bases[n])
        work[n, :, 0:64] = gram
        h_mine[n] = tn(leaf_transfer[n], nn(gram, leaf_transfer[n]))
    to_sibling = remote(h_mine, h_theirs, pair_sem.at[0], pair_sem.at[1], sibling)
    to_sibling.start()

    for panel in range(4):
        eliminate_panel(work, 0, 8, panel)

    to_sibling.wait()
    loads[2].wait()
    for n in range(8):
        work[8 + n, :, 0:64] = h_mine[n] + h_theirs[n]
    for n in range(4):
        mid = work[8 + parity * 4 + n][:, 0:64]
        k_mine[n] = tn(top_transfer[n], nn(mid, top_transfer[n]))
    to_cousin = remote(k_mine, k_theirs, pair_sem.at[2], pair_sem.at[3], cousin)
    to_cousin.start()

    for panel in range(4, 8):
        eliminate_panel(work, 0, 8, panel)

    def pair_of(first, second):
        both = jnp.where(low_lane, first, pltpu.roll(second, 64, 1))
        return jnp.where(keep, both, 0.0).astype(BF16)

    for g in range(2):
        f0, f1, f2, f3 = (work[4 * g + i] for i in range(4))
        tile = row_of(b, a) * 6 + 3 * g
        table[tile] = pair_of(f0, f1)[0:32]
        table[tile + 1] = pair_of(f2, f3)[0:32]
        corner = jnp.where(
            lane32 < 64,
            jnp.where(lane32 < 32, pltpu.roll(f0[32:64], 96, 1), f1[32:64]),
            jnp.where(lane32 < 96, pltpu.roll(f2[32:64], 32, 1), pltpu.roll(f3[32:64], 64, 1)),
        )
        table[tile + 2] = jnp.where(row32 <= lane32 % 32, corner, 0.0).astype(BF16)

    def own_sends(span, send, recv):
        for k in (4, 3, 5, 2, 6, 1, 7):
            go(remote(span, span, send.at[k], recv.at[k], device(wrap(a + k), b)))

    def own_arrivals(span_of, send, recv):
        for k in range(1, RING):
            span = span_of(wrap(a - k))
            remote(span, span, send.at[k], recv.at[k], sibling).wait_recv()

    def leaf_item(a_at):
        return table.at[pl.ds(row_of(b, a_at) * 6, 6)]

    def top_item(a_at):
        return top_table.at[row_of(b, a_at)]

    def span_at(place, piece, part=None):
        if piece < 2:
            return table.at[pl.ds((place + 4 * piece) * 6, 24)]
        low, size = (0, 8) if part is None else (4 * part, 4)
        return top_table.at[pl.ds(place + low, size)]

    def carried(h, piece, way):
        return h < 4 or piece == 2 or piece == (0 if way > 0 else 1)

    def b_span(h, piece, way):
        part = None if h < 4 else (0 if way > 0 else 1)
        return span_at(row_of(wrap(b - way * h), 0), piece, part)

    def b_slot(h, piece, way):
        return ((h - 1) * 2 + (way > 0)) * 3 + piece

    def forward(h, piece):
        for way in (1, -1):
            if carried(h + 1, piece, way):
                place = row_of(wrap(b - way * h), 0)
                part = None if h + 1 < 4 else (0 if way > 0 else 1)
                span = span_at(place, piece, part)
                slot = b_slot(h + 1, piece, way)
                to = b_right if way > 0 else b_left
                go(remote(span, span, b_send.at[slot], b_recv.at[slot], to))

    def arrive(h, piece):
        for way in (1, -1):
            if carried(h, piece, way):
                span = b_span(h, piece, way)
                slot = b_slot(h, piece, way)
                remote(span, span, b_send.at[slot], b_recv.at[slot], sibling).wait_recv()

    b_offsets = [0, -1, 1, -2, 2, -3, 3, 4]

    def hand_over(h, piece):
        for slot, offset in enumerate(b_offsets):
            if abs(offset) == h:
                span = span_at(row_of(wrap(b + offset), 0), piece)
                at = slot * 3 + piece
                go(remote(span, span, s_send.at[at], s_recv.at[at], sibling))

    def handed(piece):
        for slot, offset in enumerate(b_offsets):
            span = span_at((1 - core) * 64 + wrap(a + offset) * RING, piece)
            at = slot * 3 + piece
            remote(span, span, s_send.at[at], s_recv.at[at], sibling).wait_recv()

    def second_ring(h, piece):
        if h > 0:
            arrive(h, piece)
        if h < 4:
            forward(h, piece)
        hand_over(h, piece)

    def factor(n):
        return jnp.where(keep, work[n], 0.0)[:, 0:64]

    def inverse_transposed(n):
        return work[n][:, 64:128]

    def finish_bases():
        for k in range(2):
            at = near * 2 + k
            leaf_bases[k] = nt(bases[at], inverse_transposed(at))

    def finish_leaf(n):
        piece = nn(factor(n), leaf_transfer[n])
        leaf_transfers[n] = nt(piece, inverse_transposed(8 + n))

    def finish_top(n):
        piece = nn(factor(8 + parity * 4 + n), top_transfer[n])
        top_transfers[n] = nt(piece, inverse_transposed(16 + n))

    def stack_factors():
        for n in range(8):
            low = factor(n).astype(BF16)
            stacked[n] = jnp.concatenate([low[:, :32], low[:, 32:]], 0)

    def unpack_blocks(first, last):
        for k in range(first, last):
            slab = jnp.concatenate([couplings[k].astype(F32), couplings[k + 32].astype(F32)], 0)
            blocks[pl.ds(k, 128, stride=32), :] = jnp.transpose(slab)

    def half_step(first, last):
        for n in range(first, last):
            block = blocks[32 * n : 32 * n + 32, :].astype(BF16)
            both = nn(stacked[coupling_target[n]], block, None)
            mixed = jnp.where(low_lane, both[0:64], both[64:128])
            mixed = mixed + pltpu.roll(mixed, 64, 1)
            right = jnp.where((lane // 32) % 2 == 1, mixed, pltpu.roll(mixed, 32, 1))
            local = coupling_local[n] & 3
            mixed = jnp.where(lane // 64 == (local & 1), mixed, 0.0)
            right = jnp.where(lane // 32 == local, right, 0.0)
            halves[n, :, 0:128] = mixed.astype(BF16)
            halves[n, :, 128:256] = right.astype(BF16)

    own_sends(leaf_item(a), a_send, a_recv)

    to_cousin.wait()
    for n in range(4):
        work[16 + n, :, 0:64] = k_mine[n] + k_theirs[n]
    for panel in range(8):
        eliminate_panel(work, 8, 12, panel)
        if panel == 5:
            own_arrivals(leaf_item, a_send, a_recv)
            second_ring(0, 0)
            second_ring(0, 1)

    top_table[row_of(b, a)] = pair_of(work[16 + upper * 2], work[17 + upper * 2])
    own_sends(top_item(a), ta_send, ta_recv)

    for copy in loads[3:]:
        copy.wait()
    stack_factors()

    queue = [functools.partial(unpack_blocks, k, k + 8) for k in range(0, 32, 8)]
    queue += [functools.partial(half_step, n, n + 32) for n in range(0, 128, 32)]
    queue += [finish_bases]
    queue += [functools.partial(finish_leaf, n) for n in range(8)]
    queue += [functools.partial(finish_top, n) for n in range(4)]

    def top_hop_zero():
        own_arrivals(top_item, ta_send, ta_recv)
        second_ring(0, 2)

    events = [functools.partial(second_ring, 1, 0), functools.partial(second_ring, 1, 1), top_hop_zero]
    for h in range(2, 5):
        events += [functools.partial(second_ring, h, 0), functools.partial(second_ring, h, 1)]
        events += [functools.partial(second_ring, h - 1, 2)]
    events += [functools.partial(second_ring, 4, 2)]
    for event in events:
        event()
        for _ in range(2):
            if queue:
                queue.pop(0)()
    while queue:
        queue.pop(0)()

    handed(0)
    handed(1)

    def table_row(leaf_place):
        c = leaf_place & 1
        y_at = (leaf_place >> 1) & 7
        z_at = leaf_place >> 4
        return c * 64 + (y_at + c * (z_at - y_at)) * RING + z_at + c * (y_at - z_at)

    empty = jnp.zeros((32, 128), BF16)
    for n in range(128):
        local = coupling_local[n]
        tile = table_row(coupling_dest[n]) * 6 + (local >> 2) * 3
        upper_rows = jnp.concatenate([table[tile + ((local >> 1) & 1)], empty], 1)
        lower_rows = jnp.concatenate([empty, table[tile + 2]], 1)
        new = nt(halves[n], jnp.concatenate([upper_rows, lower_rows], 0), None)
        blocks[32 * n : 32 * n + 32, :] = jnp.concatenate([new[0:32], new[32:64]], 1)
    for k in range(32):
        slab = jnp.transpose(blocks[pl.ds(k, 128, stride=32), :]).astype(BF16)
        new_couplings[k] = slab[0:64]
        new_couplings[k + 32] = slab[64:128]

    handed(2)
    quad = me // 4

    def top_tile(cluster):
        place = (cluster >> 3) * 4 + (cluster & 2) + ((cluster >> 2) & 1)
        return top_table[table_row(place)]

    for n in range(16):
        target = quad * 8 + top_target[n]
        source = top_source[n]
        left = jnp.where((lane // 64) == (target & 1), top_tile(target), jnp.zeros((), BF16))
        block = top_couplings[n]
        double = jnp.concatenate([block, block], 1)
        half = nn(left, jnp.concatenate([double, double], 0), None)
        half = jnp.where((lane // 64) == (source & 1), half, 0.0).astype(BF16)
        new_top[n] = nt(half, top_tile(source), None).astype(BF16)

    for copy in started:
        copy.wait_send()


def hand_out(*refs):
    count = len(refs) // 2
    sems = refs[-1]
    copies = [
        pltpu.make_async_copy(refs[n], refs[count + n], sems.at[n]) for n in range(count)
    ]
    for copy in copies:
        copy.start()
    for copy in copies:
        copy.wait()


def on_device(
    bases,
    leaf_transfer,
    top_transfer,
    couplings,
    coupling_target,
    coupling_dest,
    coupling_local,
    top_couplings,
    top_target,
    top_source,
):
    vmem = pl.BlockSpec(memory_space=pltpu.VMEM)
    anywhere = pl.BlockSpec(memory_space=pl.ANY)
    dma = pltpu.SemaphoreType.DMA
    shapes = (
        jax.ShapeDtypeStruct((2, 64, 64), F32),
        jax.ShapeDtypeStruct((8, 64, 64), F32),
        jax.ShapeDtypeStruct((4, 64, 64), F32),
        jax.ShapeDtypeStruct((64, 64, 128), BF16),
        jax.ShapeDtypeStruct((16, 64, 64), BF16),
    )
    results = pl.pallas_call(
        kernel,
        out_shape=shapes,
        in_specs=[anywhere] * 10,
        out_specs=[vmem] * 5,
        scratch_shapes=[
            pltpu.VMEM((8, 64, 64), F32),
            pltpu.VMEM((8, 64, 64), F32),
            pltpu.VMEM((4, 64, 64), F32),
            pltpu.VMEM((64, 64, 128), BF16),
            pltpu.VMEM((16, 64, 64), BF16),
            pltpu.SMEM((128,), jnp.int32),
            pltpu.SMEM((128,), jnp.int32),
            pltpu.SMEM((128,), jnp.int32),
            pltpu.SMEM((16,), jnp.int32),
            pltpu.SMEM((16,), jnp.int32),
            pltpu.VMEM((20, 64, 128), F32),
            pltpu.VMEM((8, 64, 64), F32),
            pltpu.VMEM((8, 64, 64), F32),
            pltpu.VMEM((4, 64, 64), F32),
            pltpu.VMEM((4, 64, 64), F32),
            pltpu.VMEM((768, 32, 128), BF16),
            pltpu.VMEM((128, 64, 128), BF16),
            pltpu.VMEM((8, 128, 32), BF16),
            pltpu.VMEM((4096, 128), F32),
            pltpu.VMEM((128, 64, 256), BF16),
            dma((10,)),
            dma((4,)),
            dma((8,)),
            dma((8,)),
            dma((8,)),
            dma((8,)),
            dma((24,)),
            dma((24,)),
            dma((24,)),
            dma((24,)),
        ],
        compiler_params=pltpu.CompilerParams(
            collective_id=0, has_side_effects=True, vmem_limit_bytes=58 * 2**20
        ),
    )(
        bases,
        leaf_transfer,
        top_transfer,
        jnp.transpose(couplings, (1, 2, 0)),
        top_couplings,
        coupling_target,
        coupling_dest[:, 0],
        coupling_local,
        top_target,
        top_source,
    )
    leaf_bases, leaf_transfers, top_transfers, new_couplings, new_top = pl.pallas_call(
        hand_out,
        out_shape=shapes,
        in_specs=[anywhere] * 5,
        out_specs=[anywhere] * 5,
        scratch_shapes=[dma((5,))],
    )(*results)
    return (
        leaf_bases,
        leaf_transfers,
        top_transfers,
        jnp.transpose(new_couplings, (2, 0, 1)),
        new_top,
    )


def solution(mesh):
    in_specs = (
        P("leaf", None, None),
        P("leaf", None, None),
        P("leaf", None, None),
        P(("leaf", "near"), None, None),
        P(("leaf", "near")),
        P(("leaf", "near"), None),
        P(("leaf", "near")),
        P(("leaf", "near"), None, None),
        P(("leaf", "near")),
        P(("leaf", "near")),
    )
    out_specs = (
        P(("leaf", "near"), None, None),
        P("leaf", None, None),
        P("leaf", None, None),
        P(("leaf", "near"), None, None),
        P(("leaf", "near"), None, None),
    )
    return jax.shard_map(
        on_device, mesh=mesh, in_specs=in_specs, out_specs=out_specs, check_vma=False
    )
```

time: 85.3 us -> 118 us (1.38)
  Pallas kernels: 75 us -> 117 us
  local copies, waits for them, and re-layouts: 9.31 us -> 0 us
    pallas_call x1 -> x2, Pallas kernels: 75 us -> 117 us  [the longest x1 61.8 us: on_device(): pl.pallas_call(kernel, out_shape=shapes, in_specs=[anywhere] * 10, out_sp...]
    unnamed x25 -> x0, local copies, waits for them, and re-layouts: 9.31 us -> none
where the time goes in v2:
time: 118 us; the launch traced here: 117 us
  Pallas kernels  117 us (99%)
    pallas_call x1, Pallas kernels, on_device(): pl.pallas_call(kernel, out_shape=shapes, in_specs=[anywhere] * 10, out_sp...  61.8 us
    pallas_call x1, Pallas kernels, on_device(): pl.pallas_call(hand_out, out_shape=shapes, in_specs=[anywhere] * 5, out_s...  54.8 us

profile of v2, /device:TPU:1, one launch (start us, length us, event | category | flops | bytes accessed | tf_op | source)
XLA Modules:
  0.0 117.3 jit_solution(15484542352201641849)
XLA Ops:
  0.6 61.8 %shard_map.137 = (f32[2,64,64]{2,1,0:T(8,128)}, f32[8,64,64]{2,1,0:T(8,128)}, f32[4,64,64]{2,1,0:T(8,128)}, bf16[64,64,128]{2,1,0:T(8,128)(2,1)}, bf16[16,64,64]{2,1,0:T(8,128)(2,1)}) custom-call(f32[8,64,64]{2,1,0:T(8,128)} %bases_in.1, f32[8,64,64]{2,1,0:T(8,128)} %leaf_transfer_in.1, f32[4,64,64]{2,1,0:T(8,128)} %top_transfer_in.1, ...), custom_call_target="tpu_custom_call" | custom-call | tf_op jit(solution)/shard_map/pallas_call | solution.py:474
  62.4 54.8 %shard_map.138 = (f32[2,64,64]{2,1,0:T(8,128)}, f32[8,64,64]{2,1,0:T(8,128)}, f32[4,64,64]{2,1,0:T(8,128)}, bf16[64,64,128]{2,1,0:T(8,128)(2,1)}, bf16[16,64,64]{2,1,0:T(8,128)(2,1)}) custom-call(f32[2,64,64]{2,1,0:T(8,128)} %get-tuple-element.15.refs_0_, f32[8,64,64]{2,1,0:T(8,128)} %get-tuple-element.16.refs_1_, f32[4,64,64]{2,1,0:T(8,128)} %get-tuple-element.17.refs_2_, ...), custom_call_target="tpu_custom_call" | custom-call | tf_op jit(solution)/shard_map/pallas_call | solution.py:526

commit v3 on v2

--- a/solution.py
+++ b/solution.py
@@ -168,7 +168,6 @@
     partners = [sibling, b_right, b_left] + [device(wrap(a + k), b) for k in range(1, RING)]
     for partner in partners:
         pl.semaphore_signal(barrier, inc=1, device_id=partner, device_id_type=MESH)
-    pl.semaphore_wait(barrier, len(partners))
 
     def remote(source, target, send, recv, to):
         return pltpu.make_async_remote_copy(
@@ -205,6 +204,7 @@
         gram = tn(bases[n], bases[n])
         work[n, :, 0:64] = gram
         h_mine[n] = tn(leaf_transfer[n], nn(gram, leaf_transfer[n]))
+    pl.semaphore_wait(barrier, len(partners))
     to_sibling = remote(h_mine, h_theirs, pair_sem.at[0], pair_sem.at[1], sibling)
     to_sibling.start()
 
@@ -244,8 +244,11 @@
         for k in (4, 3, 5, 2, 6, 1, 7):
             go(remote(span, span, send.at[k], recv.at[k], device(wrap(a + k), b)))
 
-    def own_arrivals(span_of, send, recv):
-        for k in range(1, RING):
+    offsets = [0, 1, -1, 2, -2, 3, -3, 4]
+
+    def own_arrival(w, span_of, send, recv):
+        if w > 0:
+            k = offsets[w] % RING
             span = span_of(wrap(a - k))
             remote(span, span, send.at[k], recv.at[k], sibling).wait_recv()
 
@@ -255,60 +258,72 @@
     def top_item(a_at):
         return top_table.at[row_of(b, a_at)]
 
-    def span_at(place, piece, part=None):
-        if piece < 2:
-            return table.at[pl.ds((place + 4 * piece) * 6, 24)]
+    def span_at(b_at, piece, part=None):
+        if piece < 8:
+            return table.at[pl.ds(row_of(b_at, wrap(a - offsets[piece])) * 6, 6)]
         low, size = (0, 8) if part is None else (4 * part, 4)
-        return top_table.at[pl.ds(place + low, size)]
-
-    def carried(h, piece, way):
-        return h < 4 or piece == 2 or piece == (0 if way > 0 else 1)
-
-    def b_span(h, piece, way):
-        part = None if h < 4 else (0 if way > 0 else 1)
-        return span_at(row_of(wrap(b - way * h), 0), piece, part)
+        return top_table.at[pl.ds(row_of(b_at, 0) + low, size)]
+
+    def hop(h, piece, way):
+        if h == 4 and piece < 8 and (piece % 2 == 0) != (way > 0):
+            return None
+        return h, piece, (way < 0) * 1 if h == 4 else None
 
     def b_slot(h, piece, way):
-        return ((h - 1) * 2 + (way > 0)) * 3 + piece
+        return ((h - 1) * 2 + (way > 0)) * 9 + piece
 
     def forward(h, piece):
         for way in (1, -1):
-            if carried(h + 1, piece, way):
-                place = row_of(wrap(b - way * h), 0)
-                part = None if h + 1 < 4 else (0 if way > 0 else 1)
-                span = span_at(place, piece, part)
+            kind = hop(h + 1, piece, way)
+            if kind is not None:
+                span = span_at(wrap(b - way * h), piece, kind[2])
                 slot = b_slot(h + 1, piece, way)
                 to = b_right if way > 0 else b_left
                 go(remote(span, span, b_send.at[slot], b_recv.at[slot], to))
 
     def arrive(h, piece):
         for way in (1, -1):
-            if carried(h, piece, way):
-                span = b_span(h, piece, way)
+            kind = hop(h, piece, way)
+            if kind is not None:
+                span = span_at(wrap(b - way * h), piece, kind[2])
                 slot = b_slot(h, piece, way)
                 remote(span, span, b_send.at[slot], b_recv.at[slot], sibling).wait_recv()
 
     b_offsets = [0, -1, 1, -2, 2, -3, 3, 4]
 
-    def hand_over(h, piece):
+    def row_span(place, part):
+        if part < 2:
+            return table.at[pl.ds((place + 4 * part) * 6, 24)]
+        return top_table.at[pl.ds(place, 8)]
+
+    def hand_over(h, part):
         for slot, offset in enumerate(b_offsets):
             if abs(offset) == h:
-                span = span_at(row_of(wrap(b + offset), 0), piece)
-                at = slot * 3 + piece
+                span = row_span(row_of(wrap(b + offset), 0), part)
+                at = slot * 3 + part
                 go(remote(span, span, s_send.at[at], s_recv.at[at], sibling))
 
-    def handed(piece):
+    def handed(part):
         for slot, offset in enumerate(b_offsets):
-            span = span_at((1 - core) * 64 + wrap(a + offset) * RING, piece)
-            at = slot * 3 + piece
+            span = row_span((1 - core) * 64 + wrap(a + offset) * RING, part)
+            at = slot * 3 + part
             remote(span, span, s_send.at[at], s_recv.at[at], sibling).wait_recv()
 
     def second_ring(h, piece):
         if h > 0:
             arrive(h, piece)
+        elif piece < 8:
+            own_arrival(piece, leaf_item, a_send, a_recv)
+        else:
+            for w in range(8):
+                own_arrival(w, top_item, ta_send, ta_recv)
         if h < 4:
             forward(h, piece)
-        hand_over(h, piece)
+        if piece == 7:
+            hand_over(h, 0)
+            hand_over(h, 1)
+        elif piece == 8:
+            hand_over(h, 2)
 
     def factor(n):
         return jnp.where(keep, work[n], 0.0)[:, 0:64]
@@ -359,10 +374,12 @@
         work[16 + n, :, 0:64] = k_mine[n] + k_theirs[n]
     for panel in range(8):
         eliminate_panel(work, 8, 12, panel)
+        if panel == 3:
+            for piece in range(5):
+                second_ring(0, piece)
         if panel == 5:
-            own_arrivals(leaf_item, a_send, a_recv)
-            second_ring(0, 0)
-            second_ring(0, 1)
+            for piece in range(5, 8):
+                second_ring(0, piece)
 
     top_table[row_of(b, a)] = pair_of(work[16 + upper * 2], work[17 + upper * 2])
     own_sends(top_item(a), ta_send, ta_recv)
@@ -371,26 +388,20 @@
         copy.wait()
     stack_factors()
 
-    queue = [functools.partial(unpack_blocks, k, k + 8) for k in range(0, 32, 8)]
-    queue += [functools.partial(half_step, n, n + 32) for n in range(0, 128, 32)]
+    queue = [functools.partial(unpack_blocks, k, k + 4) for k in range(0, 32, 4)]
+    queue += [functools.partial(half_step, n, n + 8) for n in range(0, 128, 8)]
     queue += [finish_bases]
     queue += [functools.partial(finish_leaf, n) for n in range(8)]
     queue += [functools.partial(finish_top, n) for n in range(4)]
 
-    def top_hop_zero():
-        own_arrivals(top_item, ta_send, ta_recv)
-        second_ring(0, 2)
-
-    events = [functools.partial(second_ring, 1, 0), functools.partial(second_ring, 1, 1), top_hop_zero]
-    for h in range(2, 5):
-        events += [functools.partial(second_ring, h, 0), functools.partial(second_ring, h, 1)]
-        events += [functools.partial(second_ring, h - 1, 2)]
-    events += [functools.partial(second_ring, 4, 2)]
-    for event in events:
-        event()
-        for _ in range(2):
-            if queue:
-                queue.pop(0)()
+    events = [(1, w) for w in range(8)] + [(0, 8)]
+    events += [(2, w) for w in range(4)] + [(1, 8)] + [(2, w) for w in range(4, 8)]
+    events += [(3, w) for w in range(4)] + [(2, 8)] + [(3, w) for w in range(4, 8)]
+    events += [(3, 8)] + [(4, w) for w in range(8)] + [(4, 8)]
+    for h, piece in events:
+        second_ring(h, piece)
+        if queue:
+            queue.pop(0)()
     while queue:
         queue.pop(0)()
 
@@ -503,8 +514,8 @@
             dma((8,)),
             dma((8,)),
             dma((8,)),
-            dma((24,)),
-            dma((24,)),
+            dma((72,)),
+            dma((72,)),
             dma((24,)),
             dma((24,)),
         ],
@@ -526,7 +537,7 @@
     leaf_bases, leaf_transfers, top_transfers, new_couplings, new_top = pl.pallas_call(
         hand_out,
         out_shape=shapes,
-        in_specs=[anywhere] * 5,
+        in_specs=[vmem] * 5,
         out_specs=[anywhere] * 5,
         scratch_shapes=[dma((5,))],
     )(*results)

time: 118 us -> 63.7 us (0.54)
  Pallas kernels: 117 us -> 62.7 us
    pallas_call x1, Pallas kernels: 54.8 us -> 2.65 us  [on_device(): pl.pallas_call(hand_out, out_shape=shapes, in_specs=[vmem] * 5, out_specs...]
    pallas_call x1, Pallas kernels: 61.8 us -> 60 us  [on_device(): pl.pallas_call(kernel, out_shape=shapes, in_specs=[anywhere] * 10, out_sp...]
where the time goes in v3:
time: 63.7 us; the launch traced here: 63.5 us
  Pallas kernels  62.7 us (98%)
  between operations  0.8 us (1%)
    pallas_call x1, Pallas kernels, on_device(): pl.pallas_call(kernel, out_shape=shapes, in_specs=[anywhere] * 10, out_sp...  60 us
    pallas_call x1, Pallas kernels, on_device(): pl.pallas_call(hand_out, out_shape=shapes, in_specs=[vmem] * 5, out_specs...  2.65 us

profile of v3, /device:TPU:1, one launch (start us, length us, event | category | flops | bytes accessed | tf_op | source)
XLA Modules:
  0.0 63.5 jit_solution(11320915686615983859)
XLA Ops:
  0.6 60.0 %shard_map.137 = (f32[2,64,64]{2,1,0:T(8,128)}, f32[8,64,64]{2,1,0:T(8,128)}, f32[4,64,64]{2,1,0:T(8,128)}, bf16[64,64,128]{2,1,0:T(8,128)(2,1)}, bf16[16,64,64]{2,1,0:T(8,128)(2,1)}) custom-call(f32[8,64,64]{2,1,0:T(8,128)} %bases_in.1, f32[8,64,64]{2,1,0:T(8,128)} %leaf_transfer_in.1, f32[4,64,64]{2,1,0:T(8,128)} %top_transfer_in.1, ...), custom_call_target="tpu_custom_call" | custom-call | tf_op jit(solution)/shard_map/pallas_call | solution.py:485
  60.7 2.6 %shard_map.138 = (f32[2,64,64]{2,1,0:T(8,128)}, f32[8,64,64]{2,1,0:T(8,128)}, f32[4,64,64]{2,1,0:T(8,128)}, bf16[64,64,128]{2,1,0:T(8,128)(2,1)}, bf16[16,64,64]{2,1,0:T(8,128)(2,1)}) custom-call(f32[2,64,64]{2,1,0:T(8,128)} %get-tuple-element.15.refs_0_, f32[8,64,64]{2,1,0:T(8,128)} %get-tuple-element.16.refs_1_, f32[4,64,64]{2,1,0:T(8,128)} %get-tuple-element.17.refs_2_, ...), custom_call_target="tpu_custom_call" | custom-call | tf_op jit(solution)/shard_map/pallas_call | solution.py:537

commit v4 on v3

--- a/solution.py
+++ b/solution.py
@@ -241,7 +241,7 @@
         table[tile + 2] = jnp.where(row32 <= lane32 % 32, corner, 0.0).astype(BF16)
 
     def own_sends(span, send, recv):
-        for k in (4, 3, 5, 2, 6, 1, 7):
+        for k in (1, 7, 2, 6, 3, 5, 4):
             go(remote(span, span, send.at[k], recv.at[k], device(wrap(a + k), b)))
 
     offsets = [0, 1, -1, 2, -2, 3, -3, 4]
@@ -368,18 +368,13 @@
             halves[n, :, 128:256] = right.astype(BF16)
 
     own_sends(leaf_item(a), a_send, a_recv)
+    second_ring(0, 0)
 
     to_cousin.wait()
     for n in range(4):
         work[16 + n, :, 0:64] = k_mine[n] + k_theirs[n]
     for panel in range(8):
-        eliminate_panel(work, 8, 12, panel)
-        if panel == 3:
-            for piece in range(5):
-                second_ring(0, piece)
-        if panel == 5:
-            for piece in range(5, 8):
-                second_ring(0, piece)
+        eliminate_panel(work, 16, 4, panel)
 
     top_table[row_of(b, a)] = pair_of(work[16 + upper * 2], work[17 + upper * 2])
     own_sends(top_item(a), ta_send, ta_recv)
@@ -390,14 +385,17 @@
 
     queue = [functools.partial(unpack_blocks, k, k + 4) for k in range(0, 32, 4)]
     queue += [functools.partial(half_step, n, n + 8) for n in range(0, 128, 8)]
+    queue += [functools.partial(eliminate_panel, work, 8, 8, panel) for panel in range(8)]
     queue += [finish_bases]
     queue += [functools.partial(finish_leaf, n) for n in range(8)]
     queue += [functools.partial(finish_top, n) for n in range(4)]
 
-    events = [(1, w) for w in range(8)] + [(0, 8)]
-    events += [(2, w) for w in range(4)] + [(1, 8)] + [(2, w) for w in range(4, 8)]
-    events += [(3, w) for w in range(4)] + [(2, 8)] + [(3, w) for w in range(4, 8)]
-    events += [(3, 8)] + [(4, w) for w in range(8)] + [(4, 8)]
+    leaf_events = [(h, w) for h in range(5) for w in range(8)][1:]
+    events = []
+    for h, w in sorted(leaf_events, key=lambda at: (at[1] + 6 * at[0], -at[0])):
+        events.append((h, w))
+        if w == 7:
+            events.append((h, 8))
     for h, piece in events:
         second_ring(h, piece)
         if queue:

time: 63.7 us -> 60.8 us (0.954)
  Pallas kernels: 62.7 us -> 59.8 us
    pallas_call x1, Pallas kernels: 60 us -> 57.2 us  [on_device(): pl.pallas_call(kernel, out_shape=shapes, in_specs=[anywhere] * 10, out_sp...]
where the time goes in v4:
time: 60.8 us; the launch traced here: 60.6 us
  Pallas kernels  59.8 us (98%)
  between operations  0.8 us (1%)
    pallas_call x1, Pallas kernels, on_device(): pl.pallas_call(kernel, out_shape=shapes, in_specs=[anywhere] * 10, out_sp...  57.2 us
    pallas_call x1, Pallas kernels, on_device(): pl.pallas_call(hand_out, out_shape=shapes, in_specs=[vmem] * 5, out_specs...  2.65 us

profile of v4, /device:TPU:1, one launch (start us, length us, event | category | flops | bytes accessed | tf_op | source)
XLA Modules:
  0.0 60.6 jit_solution(12057528988143956739)
XLA Ops:
  0.6 57.2 %shard_map.137 = (f32[2,64,64]{2,1,0:T(8,128)}, f32[8,64,64]{2,1,0:T(8,128)}, f32[4,64,64]{2,1,0:T(8,128)}, bf16[64,64,128]{2,1,0:T(8,128)(2,1)}, bf16[16,64,64]{2,1,0:T(8,128)(2,1)}) custom-call(f32[8,64,64]{2,1,0:T(8,128)} %bases_in.1, f32[8,64,64]{2,1,0:T(8,128)} %leaf_transfer_in.1, f32[4,64,64]{2,1,0:T(8,128)} %top_transfer_in.1, ...), custom_call_target="tpu_custom_call" | custom-call | tf_op jit(solution)/shard_map/pallas_call | solution.py:483
  57.8 2.6 %shard_map.138 = (f32[2,64,64]{2,1,0:T(8,128)}, f32[8,64,64]{2,1,0:T(8,128)}, f32[4,64,64]{2,1,0:T(8,128)}, bf16[64,64,128]{2,1,0:T(8,128)(2,1)}, bf16[16,64,64]{2,1,0:T(8,128)(2,1)}) custom-call(f32[2,64,64]{2,1,0:T(8,128)} %get-tuple-element.15.refs_0_, f32[8,64,64]{2,1,0:T(8,128)} %get-tuple-element.16.refs_1_, f32[4,64,64]{2,1,0:T(8,128)} %get-tuple-element.17.refs_2_, ...), custom_call_target="tpu_custom_call" | custom-call | tf_op jit(solution)/shard_map/pallas_call | solution.py:535

commit v5 on v4

--- a/solution.py
+++ b/solution.py
@@ -394,8 +394,11 @@
     events = []
     for h, w in sorted(leaf_events, key=lambda at: (at[1] + 6 * at[0], -at[0])):
         events.append((h, w))
-        if w == 7:
-            events.append((h, 8))
+        if h == 0 and w == 7:
+            events.append((0, 8))
+        if h > 1 and w == 3:
+            events.append((h - 1, 8))
+    events.append((4, 8))
     for h, piece in events:
         second_ring(h, piece)
         if queue:
@@ -447,15 +450,23 @@
 
 
 def hand_out(*refs):
-    count = len(refs) // 2
-    sems = refs[-1]
-    copies = [
-        pltpu.make_async_copy(refs[n], refs[count + n], sems.at[n]) for n in range(count)
-    ]
-    for copy in copies:
-        copy.start()
-    for copy in copies:
-        copy.wait()
+    sources, targets, held = refs[0:5], refs[5:10], refs[10:15]
+    in_sem, out_sem = refs[15:]
+    pieces = [(3, pl.ds(16 * n, 16)) for n in range(4)]
+    pieces += [(n, pl.ds(0, sources[n].shape[0])) for n in (1, 4, 2, 0)]
+    arrivals, departures = [], []
+    for at, (n, span) in enumerate(pieces):
+        inward = pltpu.make_async_copy(sources[n].at[span], held[n].at[span], in_sem.at[at])
+        inward.start()
+        arrivals.append(inward)
+        departures.append(
+            pltpu.make_async_copy(held[n].at[span], targets[n].at[span], out_sem.at[at])
+        )
+    for inward, outward in zip(arrivals, departures):
+        inward.wait()
+        outward.start()
+    for outward in departures:
+        outward.wait()
 
 
 def on_device(
@@ -535,9 +546,11 @@
     leaf_bases, leaf_transfers, top_transfers, new_couplings, new_top = pl.pallas_call(
         hand_out,
         out_shape=shapes,
-        in_specs=[vmem] * 5,
+        in_specs=[anywhere] * 5,
         out_specs=[anywhere] * 5,
-        scratch_shapes=[dma((5,))],
+        scratch_shapes=[pltpu.VMEM(shape.shape, shape.dtype) for shape in shapes]
+        + [dma((8,)), dma((8,))],
+        compiler_params=pltpu.CompilerParams(vmem_limit_bytes=58 * 2**20),
     )(*results)
     return (
         leaf_bases,

time: 60.8 us -> 60.2 us (level)
  no operation moved by 1% of the time
where the time goes in v5:
time: 60.2 us; the launch traced here: 60 us
  Pallas kernels  59.2 us (98%)
  between operations  0.8 us (1%)
    pallas_call x1, Pallas kernels, on_device(): pl.pallas_call(kernel, out_shape=shapes, in_specs=[anywhere] * 10, out_sp...  56.9 us
    pallas_call x1, Pallas kernels, on_device(): pl.pallas_call(hand_out, out_shape=shapes, in_specs=[anywhere] * 5, out_s...  2.28 us

profile of v5, /device:TPU:1, one launch (start us, length us, event | category | flops | bytes accessed | tf_op | source)
XLA Modules:
  0.0 60.0 jit_solution(18125434762388935247)
XLA Ops:
  0.6 56.9 %shard_map.137 = (f32[2,64,64]{2,1,0:T(8,128)}, f32[8,64,64]{2,1,0:T(8,128)}, f32[4,64,64]{2,1,0:T(8,128)}, bf16[64,64,128]{2,1,0:T(8,128)(2,1)}, bf16[16,64,64]{2,1,0:T(8,128)(2,1)}) custom-call(f32[8,64,64]{2,1,0:T(8,128)} %bases_in.1, f32[8,64,64]{2,1,0:T(8,128)} %leaf_transfer_in.1, f32[4,64,64]{2,1,0:T(8,128)} %top_transfer_in.1, ...), custom_call_target="tpu_custom_call" | custom-call | tf_op jit(solution)/shard_map/pallas_call | solution.py:494
  57.6 2.3 %shard_map.138 = (f32[2,64,64]{2,1,0:T(8,128)}, f32[8,64,64]{2,1,0:T(8,128)}, f32[4,64,64]{2,1,0:T(8,128)}, bf16[64,64,128]{2,1,0:T(8,128)(2,1)}, bf16[16,64,64]{2,1,0:T(8,128)(2,1)}) custom-call(f32[2,64,64]{2,1,0:T(8,128)} %get-tuple-element.15.refs_0_, f32[8,64,64]{2,1,0:T(8,128)} %get-tuple-element.16.refs_1_, f32[4,64,64]{2,1,0:T(8,128)} %get-tuple-element.17.refs_2_, ...), custom_call_target="tpu_custom_call" | custom-call | tf_op jit(solution)/shard_map/pallas_call | solution.py:546
